TPU v7x, 32 devices: a whole 2x2x4 slice. The times are simulated.
32 devices in a mesh: tm: 4 (over y, x), pts: 8 (over z, core).
Axes of the slice: x: 2, y: 2, z: 4, core: 2. Of those that a mesh axis runs over, the one named last changes fastest.
Arguments:
- orbitals: bfloat16 [8192, 2048], P('pts'), may hold values from -6 to 6
- panel_orbitals: bfloat16 [1024, 2048], P(('tm', 'pts')), may hold values from -0.1796875 to 0.1796875
- band_gap: float32 [2048], replicated, may hold values from 0.1 to 1
- tau_points: float32 [4], replicated, may hold values from 0.1 to 2
- quad_weight: float32 [4], replicated, may hold values from 0.1 to 1
- frequencies: float32 [8], replicated, may hold values from 0.1 to 3
- coulomb: bfloat16 [1024, 1024], P(('tm', 'pts')), may hold values from -0.1875 to 0.1875
Outputs:
- screened: bfloat16 [8, 8192, 1024], P(None, ('pts', 'tm'))
All inputs are finite; a program needn't handle non-finite values.
Results may differ from a plain program's by a relative error of at most 0.0056.
Values may be sent and summed in bfloat16 or wider, within the bound.
A program may use at most 64 MiB of HBM per device.

v0:
```python
import jax
import jax.numpy as jnp
from jax import lax
from jax.sharding import PartitionSpec as P

NOCC = 512
PANEL = 1024
TAU_DEV = 1
FREQS = 8


def contract(left, right):
    return lax.dot_general(
        left, right, (((1,), (1,)), ((), ())), preferred_element_type=jnp.float32
    )


def shards(orbitals, panel_orbitals, band_gap, tau_points, quad_weight, frequencies, coulomb):
    group = lax.axis_index("tm")
    own_taus = lax.dynamic_slice_in_dim(tau_points, group * TAU_DEV, TAU_DEV)
    decay = jnp.exp(-band_gap[None, :] * own_taus[:, None])
    occ_rows = orbitals[:, :NOCC]
    vir_rows = orbitals[:, NOCC:]
    widened = lax.all_gather(panel_orbitals, ("tm", "pts"), axis=0, tiled=True).astype(jnp.float32)
    scaled = (widened * decay[0][None, :]).astype(jnp.bfloat16)
    green_occ = contract(occ_rows, scaled[:, :NOCC])
    green_vir = contract(vir_rows, scaled[:, NOCC:])
    layers = [(-(green_occ * green_vir)).astype(jnp.bfloat16)]
    polar = jnp.stack(layers)
    regrouped = lax.all_to_all(polar, "tm", split_axis=1, concat_axis=0, tiled=True)
    times_all = regrouped.shape[0]
    row_count = regrouped.shape[1]
    cosines = quad_weight[None, :] * jnp.cos(frequencies[:, None] * tau_points[None, :])
    flat = regrouped.reshape(times_all, row_count * PANEL).astype(jnp.float32)
    transformed = jnp.dot(cosines, flat, precision=lax.Precision.HIGHEST).astype(jnp.bfloat16)
    transformed = transformed.reshape(FREQS * row_count, PANEL)
    whole_block = lax.all_gather(coulomb, ("tm", "pts"), axis=0, tiled=True)
    screened = jnp.dot(transformed, whole_block, preferred_element_type=jnp.float32)
    return screened.astype(jnp.bfloat16).reshape(FREQS, row_count, PANEL)


def solution(mesh):
    placed = (P("pts", None), P(("tm", "pts"), None), P(), P(), P(), P(), P(("tm", "pts"), None))
    return jax.shard_map(
        shards, mesh=mesh, in_specs=placed, out_specs=P(None, ("pts", "tm"), None), check_vma=False
    )
```

profile of v0, /device:TPU:1, one launch (start us, length us, event | category | flops | bytes accessed | tf_op | source)
XLA Modules:
  0.0 187.0 jit_solution(1147528016978019313)
XLA Ops:
  6.5 0.0 all-gather.3.cloned.1.call-start
  6.5 0.7 all-gather.3.cloned.1.call-update
  7.3 0.0 all-gather.5.cloned.1.call-start
  7.3 0.7 all-gather.5.cloned.1.call-update
  8.0 1.2 dynamic_slice.3
  9.3 1.3 multiply_exponential_fusion
  10.6 63.9 %all-gather.3.cloned.1.call-done = bf16[1024,2048]{1,0:T(8,128)(2,1)} async-done(((bf16[32,2048]{1,0:T(8,128)(2,1)}), bf16[1024,2048]{1,0:T(8,128)(2,1)}) %all-gather.3.cloned.1.call-update) | async-done | bytes 4194320 | tf_op jit(solution)/shard_map/all_gather | solution.py:24
  74.5 3.4 %multiply_convert_fusion = bf16[1024,2048]{1,0:T(8,128)(2,1)S(1)} fusion(bf16[1024,2048]{1,0:T(8,128)(2,1)} %all-gather.3.cloned.1.call-done, f32[2048]{0:T(1024)S(1)} %multiply_exponential_fusion), kind=kLoop, calls=%fused_computation.1 | loop fusion | flops 6291456 | bytes 8396800 | tf_op jit(solution)/shard_map/convert_element_type | solution.py:25
  78.0 0.0 copy-done
  78.0 3.4 %fusion = f32[1024,1024]{1,0:T(8,128)S(1)} fusion(bf16[1024,2048]{1,0:T(8,128)(2,1)S(1)} %multiply_convert_fusion, bf16[1024,2048]{1,0:T(8,128)(2,1)S(1)} %copy-done), kind=kOutput, calls=%fused_computation.4 | convolution fusion | flops 3221225472 | bytes 10485760 | tf_op jit(solution)/shard_map/dot_general | solution.py:13
  81.4 1.3 fusion.3
  82.8 7.5 %copy.9 = bf16[1,1024,1024]{2,0,1:T(2,128)(2,1)} copy(bf16[1,1024,1024]{1,2,0:T(8,128)(2,1)S(1)} %fusion.3) | data formatting | bytes 4194304 | tf_op jit(solution)/shard_map/stack | solution.py:29
  90.3 0.5 broadcast.7
  90.8 12.8 %reduce.2 = bf16[1024,1024]{1,0:T(8,128)(2,1)S(1)} reduce(bf16[1024,1,1024]{2,1,0:T(2,128)(2,1)} %bitcast.12, bf16[]{:T(256)} %broadcast.7), dimensions={1}, to_apply=%bitcast.6.reduce_sub_computation | reduce | bytes 4194306
  103.6 2.8 %reshape.27 = bf16[4,2,131072]{2,1,0:T(2,128)(2,1)} reshape(bf16[1024,1024]{1,0:T(8,128)(2,1)S(1)} %reduce.2) | data formatting | bytes 4194304
  106.3 32.1 %all_to_all.4 = bf16[4,2,131072]{2,1,0:T(2,128)(2,1)S(1)} all-to-all(bf16[4,2,131072]{2,1,0:T(2,128)(2,1)} %reshape.27), channel_id=1, replica_groups=mesh['tm'=4,'pts'=8] {'tm'}, dimensions={0} | all-to-all | bytes 4194304 | tf_op jit(solution)/shard_map/all_to_all | solution.py:30
  138.4 3.3 %reshape.28 = bf16[1024,1,1024]{2,1,0:T(2,128)(2,1)} reshape(bf16[4,2,131072]{2,1,0:T(2,128)(2,1)S(1)} %all_to_all.4) | data formatting | bytes 4194304
  141.7 14.7 %bitcast_reduce_fusion = bf16[1024,1024]{1,0:T(8,128)(2,1)} fusion(bf16[1024,1,1024]{2,1,0:T(2,128)(2,1)} %reshape.28), kind=kLoop, calls=%fused_computation.17 | loop fusion | bytes 4194304 | tf_op jit(solution)/shard_map/all_to_all | solution.py:30
  156.4 3.2 %reshape.23 = bf16[4,262144]{1,0:T(4,128)(2,1)S(1)} reshape(bf16[1024,1024]{1,0:T(8,128)(2,1)} %bitcast_reduce_fusion) | data formatting | bytes 4194304 | tf_op jit(solution)/shard_map/reshape | solution.py:34
  159.6 0.0 copy-done.1
  159.6 0.0 copy-done.2
  159.6 5.1 %convolution_convert_fusion = bf16[8,262144]{1,0:T(8,128)(2,1)} fusion(bf16[4,262144]{1,0:T(4,128)(2,1)S(1)} %reshape.23, f32[4]{0:T(128)S(1)} %copy-done.1, f32[8]{0:T(128)S(1)} %copy-done.2, f32[4]{0:T(128)S(1)} %copy-done.3), kind=kOutput, calls=%fused_computation | convolution fusion | flops 102760512 | bytes 6291520 | tf_op jit(solution)/shard_map/dot_general | solution.py:35
  164.8 6.0 %reshape.24 = bf16[2048,1024]{1,0:T(8,128)(2,1)} reshape(bf16[8,262144]{1,0:T(8,128)(2,1)} %convolution_convert_fusion) | data formatting | bytes 8388608 | tf_op jit(solution)/shard_map/reshape | solution.py:36
  170.8 9.4 %convolution_convert_fusion.1 = bf16[2048,1024]{1,0:T(8,128)(2,1)} fusion(bf16[2048,1024]{1,0:T(8,128)(2,1)} %reshape.24, bf16[1024,1024]{1,0:T(8,128)(2,1)} %all-gather.5.cloned.1.call-done), kind=kOutput, calls=%fused_computation.3 | convolution fusion | flops 4297064448 | bytes 10485760 | tf_op jit(solution)/shard_map/dot_general | solution.py:38
  (6 shorter events, 0.0 us)
Async XLA Ops:
  6.5 68.0 %all-gather.3.cloned.1.call-start = ((), (), s32[]{:S(2)}) async-start(), calls=%async_computation.1 | async-start | bytes 4325376 | tf_op jit(solution)/shard_map/all_gather | solution.py:24
  7.3 163.5 %all-gather.5.cloned.1.call-start = ((), (), s32[]{:S(2)}) async-start(), calls=%async_computation.2 | async-start | bytes 2162688 | tf_op jit(solution)/shard_map/all_gather | solution.py:37
  74.5 3.5 %copy-start = (bf16[1024,2048]{1,0:T(8,128)(2,1)S(1)}, bf16[1024,2048]{1,0:T(8,128)(2,1)}, u32[]{:S(2)}) copy-start(bf16[1024,2048]{1,0:T(8,128)(2,1)} %param.7) | copy-start | bytes 12582916
  141.7 17.9 %copy-start.1 = (f32[4]{0:T(128)S(1)}, f32[4]{0:T(128)}, u32[]{:S(2)}) copy-start(f32[4]{0:T(128)} %param.10) | copy-start | bytes 52
  141.7 17.9 %copy-start.2 = (f32[8]{0:T(128)S(1)}, f32[8]{0:T(128)}, u32[]{:S(2)}) copy-start(f32[8]{0:T(128)} %param.12) | copy-start | bytes 100
  141.7 17.9 %copy-start.3 = (f32[4]{0:T(128)S(1)}, f32[4]{0:T(128)}, u32[]{:S(2)}) copy-start(f32[4]{0:T(128)} %param.11) | copy-start | bytes 52
Sparse Core Ops, SparseCore 0:
  10.3 64.1 all-gather.2
  77.5 60.8 all-gather.4
where the time goes:
time: 189 us; the launch traced here: 187 us
  waiting for transfers between devices  65.3 us (35%)
  local copies, waits for them, and re-layouts  39.2 us (21%)
  blocking collectives  32.1 us (17%)
  matrix products  19.3 us (10%)
  other arithmetic  17.5 us (9%)
  between operations  13.5 us (7%)
    all_gather x1, waiting for transfers between devices, shards(): lax.all_gather(panel_orbitals, ('tm', 'pts'), axis=0, tiled=True)  63.9 us
    all_to_all x1, blocking collectives, shards(): lax.all_to_all(polar, 'tm', split_axis=1, concat_axis=0, tiled=True)  32.1 us
    all_to_all x1, local copies, waits for them, and re-layouts, shards(): lax.all_to_all(polar, 'tm', split_axis=1, concat_axis=0, tiled=True)  14.7 us
    unnamed x1, other arithmetic  12.8 us
    dot_general x1, matrix products, shards(): jnp.dot(transformed, whole_block, preferred_element_type=jnp.float32)  9.41 us
    another operation x1, local copies, waits for them, and re-layouts, shards(): polar = jnp.stack(layers)  7.52 us
    unnamed x11, local copies, waits for them, and re-layouts  6.57 us
    reshape x1, local copies, waits for them, and re-layouts, shards(): transformed = transformed.reshape(FREQS * row_count, PANEL)  6.02 us
  transfers between devices with their start and end apart: 2, of which 1 were waited for; matrix products, arithmetic and copies ran while one was open for 36% of the time, Pallas kernels for 0%

commit v1 on v0

v1 whole, which is shorter than its diff:
```python
import jax
import jax.numpy as jnp
from jax import lax
from jax.sharding import PartitionSpec as P

NOCC = 512


def contract(left, right):
    return lax.dot_general(
        left, right, (((1,), (1,)), ((), ())), preferred_element_type=jnp.float32
    )


def shards(orbitals, panel_orbitals, band_gap, tau_points, quad_weight, frequencies, coulomb):
    times = tau_points.shape[0]
    rows = orbitals.shape[0] // lax.axis_size("tm")
    own = lax.dynamic_slice_in_dim(orbitals, lax.axis_index("tm") * rows, rows)
    decay = jnp.exp(-band_gap[None, :] * tau_points[:, None])
    scaled = (own.astype(jnp.float32)[None] * decay[:, None, :]).astype(jnp.bfloat16)
    scaled = scaled.reshape(times * rows, -1)
    panel = lax.all_gather(panel_orbitals, ("tm", "pts"), axis=0, tiled=True)
    block = lax.all_gather(coulomb, ("tm", "pts"), axis=0, tiled=True)
    green_occ = contract(scaled[:, :NOCC], panel[:, :NOCC])
    green_vir = contract(scaled[:, NOCC:], panel[:, NOCC:])
    polar = (-(green_occ * green_vir)).astype(jnp.bfloat16)
    product = jnp.dot(polar, block, preferred_element_type=jnp.float32)
    product = product.reshape(times, rows, -1)
    cosines = quad_weight[None, :] * jnp.cos(frequencies[:, None] * tau_points[None, :])
    total = cosines[:, 0, None, None] * product[None, 0]
    for t in range(1, times):
        total = total + cosines[:, t, None, None] * product[None, t]
    return total.astype(jnp.bfloat16)


def solution(mesh):
    placed = (P("pts", None), P(("tm", "pts"), None), P(), P(), P(), P(), P(("tm", "pts"), None))
    return jax.shard_map(
        shards, mesh=mesh, in_specs=placed, out_specs=P(None, ("pts", "tm"), None), check_vma=False
    )
```

time: 189 us -> 155 us (0.82)
  waiting for transfers between devices: 65.3 us -> 111 us
  local copies, waits for them, and re-layouts: 39.2 us -> 2.49 us
  blocking collectives: 32.1 us -> 0 us
  other arithmetic: 17.5 us -> 10.3 us
  matrix products: 19.3 us -> 17.1 us
    all_gather x2, waiting for transfers between devices: 63.9 us -> 110 us  [the longest x1 59.7 us: shards(): panel = lax.all_gather(panel_orbitals, ('tm', 'pts'), axis=0, tiled=True)]
    all_to_all x1 -> x0, blocking collectives: 32.1 us -> none  [shards(): lax.all_to_all(polar, 'tm', split_axis=1, concat_axis=0, tiled=True)]
    all_to_all x1 -> x0, local copies, waits for them, and re-layouts: 14.7 us -> none  [shards(): lax.all_to_all(polar, 'tm', split_axis=1, concat_axis=0, tiled=True)]
    unnamed x1 -> x0, other arithmetic: 12.8 us -> none
    reshape x2 -> x0, local copies, waits for them, and re-layouts: 9.22 us -> none  [the longest x1 6.02 us: shards(): transformed = transformed.reshape(FREQS * row_count, PANEL)]
    another operation x1 -> x0, local copies, waits for them, and re-layouts: 7.52 us -> none  [shards(): polar = jnp.stack(layers)]
    unnamed x11 -> x0, local copies, waits for them, and re-layouts: 6.57 us -> none
    dot_general x2 -> x1, matrix products: 14.5 us -> 8.88 us  [shards(): product = jnp.dot(polar, block, preferred_element_type=jnp.float32)]
  transfers between devices with their start and end apart: 2 -> 2, of which waited for: 1 -> 2; matrix products, arithmetic and copies ran while one was open for 36% -> 10% of each run, Pallas kernels for 0% -> 0%
where the time goes in v1:
time: 155 us; the launch traced here: 154 us
  waiting for transfers between devices  111 us (72%)
  matrix products  17.1 us (11%)
  between operations  13.4 us (9%)
  other arithmetic  10.3 us (7%)
  local copies, waits for them, and re-layouts  2.49 us (2%)
    all_gather x1, waiting for transfers between devices, shards(): panel = lax.all_gather(panel_orbitals, ('tm', 'pts'), axis=0, tiled=True)  59.7 us
    all_gather x1, waiting for transfers between devices, shards(): block = lax.all_gather(coulomb, ('tm', 'pts'), axis=0, tiled=True)  49.9 us
    dot_general x1, matrix products, shards(): product = jnp.dot(polar, block, preferred_element_type=jnp.float32)  8.88 us
    dot_general x1, matrix products, contract(): lax.dot_general(left, right, (((1,), (1,)), ((), ())), preferred_element_...  8.27 us
    convert_element_type x1, other arithmetic, shards(): return total.astype(jnp.bfloat16)  3.58 us
  transfers between devices with their start and end apart: 2, of which 2 were waited for; matrix products, arithmetic and copies ran while one was open for 10% of the time, Pallas kernels for 0%

profile of v1, /device:TPU:1, one launch (start us, length us, event | category | flops | bytes accessed | tf_op | source)
XLA Modules:
  0.0 154.4 jit_solution(13668770092308595816)
XLA Ops:
  6.5 0.0 all-gather.3.cloned.1.call-start
  6.5 0.7 all-gather.3.cloned.1.call-update
  7.3 0.0 all-gather.5.cloned.1.call-start
  7.3 0.7 all-gather.5.cloned.1.call-update
  8.0 0.7 neg.7
  8.7 0.8 cosine_multiply_fusion
  9.5 1.5 dynamic-slice_convert_fusion
  11.0 0.7 multiply_exponential_fusion
  11.7 3.1 %multiply_convert_fusion = bf16[4,256,2048]{2,1,0:T(8,128)(2,1)} fusion(f32[4,2048]{1,0:T(4,128)S(1)} %multiply_exponential_fusion, f32[256,2048]{1,0:T(8,128)S(1)} %dynamic-slice_convert_fusion), kind=kLoop, calls=%fused_computation.1 | loop fusion | flops 4194304 | bytes 6324224 | tf_op jit(solution)/shard_map/convert_element_type | solution.py:20
  14.8 59.7 %all-gather.3.cloned.1.call-done = bf16[1024,2048]{1,0:T(8,128)(2,1)} async-done(((bf16[32,2048]{1,0:T(8,128)(2,1)}), bf16[1024,2048]{1,0:T(8,128)(2,1)}) %all-gather.3.cloned.1.call-update) | async-done | bytes 4194320 | tf_op jit(solution)/shard_map/all_gather | solution.py:22
  74.5 8.3 %fusion = f32[1024,1024]{1,0:T(8,128)} fusion(bf16[1024,2048]{1,0:T(8,128)(2,1)} %all-gather.3.cloned.1.call-done, bf16[1024,2048]{1,0:T(8,128)(2,1)} %bitcast.10), kind=kOutput, calls=%fused_computation.3 | convolution fusion | flops 3221225472 | bytes 10485760 | tf_op jit(solution)/shard_map/dot_general | solution.py:10
  82.8 49.9 %all-gather.5.cloned.1.call-done = bf16[1024,1024]{1,0:T(8,128)(2,1)} async-done(((bf16[32,1024]{1,0:T(8,128)(2,1)}), bf16[1024,1024]{1,0:T(8,128)(2,1)}) %all-gather.5.cloned.1.call-update) | async-done | bytes 2097168 | tf_op jit(solution)/shard_map/all_gather | solution.py:23
  132.7 8.9 %fusion.7 = f32[1024,1024]{1,0:T(8,128)} fusion(bf16[1024,1024]{1,0:T(8,128)(2,1)} %all-gather.5.cloned.1.call-done, f32[1024,1024]{1,0:T(8,128)} %fusion, bf16[1024,2048]{1,0:T(8,128)(2,1)} %all-gather.3.cloned.1.call-done, bf16[1024,2048]{1,0:T(8,128)(2,1)} %bitcast.11), kind=kOutput, calls=%fused_computation.9 | convolution fusion | flops 3224371200 | bytes 12582912 | tf_op jit(solution)/shard_map/dot_general | solution.py:27
  141.5 2.5 %fusion.10 = (f32[256,1024]{1,0:T(8,128)S(1)}, f32[256,1024]{1,0:T(8,128)S(1)}, f32[256,1024]{1,0:T(8,128)S(1)}, f32[256,1024]{1,0:T(8,128)S(1)}) fusion(f32[1024,1024]{1,0:T(8,128)} %fusion.7), kind=kLoop, calls=%fused_computation.16 | loop fusion | bytes 8388608 | tf_op jit(solution)/shard_map/slice | solution.py:30
  144.0 3.6 %add_convert_fusion = bf16[8,256,1024]{2,1,0:T(8,128)(2,1)} fusion(f32[256,1024]{1,0:T(8,128)S(1)} %get-tuple-element.6, f32[8]{0:T(128)S(1)} %get-tuple-element.10, f32[256,1024]{1,0:T(8,128)S(1)} %get-tuple-element.7, f32[8]{0:T(128)S(1)} %get-tuple-element.11, f32[256,1024]{1,0:T(8,128)S(1)} %get-tuple-element.8, f32[8]{0:T(128)S(1)} %get-tuple-element.12, ...), kind=kLoop, calls=%fused_computation | loop fusion | flops 16777216 | bytes 8388736 | tf_op jit(solution)/shard_map/convert_element_type | solution.py:33
  (1 shorter events, 0.0 us)
Async XLA Ops:
  6.5 68.0 %all-gather.3.cloned.1.call-start = ((), (), s32[]{:S(2)}) async-start(), calls=%async_computation | async-start | bytes 4325376 | tf_op jit(solution)/shard_map/all_gather | solution.py:22
  7.3 125.4 %all-gather.5.cloned.1.call-start = ((), (), s32[]{:S(2)}) async-start(), calls=%async_computation.1 | async-start | bytes 2162688 | tf_op jit(solution)/shard_map/all_gather | solution.py:23
Sparse Core Ops, SparseCore 0:
  10.3 64.1 all-gather.2
  77.5 55.1 all-gather.4

commit v2 on v1

v2 whole, which is shorter than its diff:
```python
import functools
import jax
import jax.numpy as jnp
from jax import lax
from jax.experimental import pallas as pl
from jax.experimental.pallas import tpu as pltpu
from jax.sharding import PartitionSpec as P

NOCC = 512
MESH = pl.DeviceIdType.MESH
DIRS = 7


def when(valid, run):
    if valid is True:
        run()
    elif valid is not False:
        pl.when(valid)(run)


def both(a, b):
    if a is True:
        return b
    if b is True:
        return a
    if a is False or b is False:
        return False
    return jnp.logical_and(a, b)


class Line:
    def __init__(self, at, size):
        self.at, self.size = at, size
        if size == 1:
            self.sends, self.arrivals, self.peers = [], [], 0
        elif size == 2:
            other = 1 - at
            self.peers = 1
            self.sends = [(0, other, True)]
            self.arrivals = [(other, True, [])]
        elif size <= 4:
            down, up = at > 0, at < size - 1
            self.peers = lax.div(at + size - 1, size) + lax.div(2 * size - 2 - at, size)
            self.sends = [(0, at - 1, down), (1, at + 1, up)]
            self.arrivals = []
            for far in range(1, size):
                self.arrivals.append((at - far, at >= far, [(1, at + 1, up)]))
                self.arrivals.append((at + far, at < size - far, [(0, at - 1, down)]))
        else:
            before, after = lax.rem(at + size - 1, size), lax.rem(at + 1, size)
            self.sends = [(0, before, True), (1, after, True)]
            self.peers = 2
            self.arrivals = []
            ups, downs = size // 2, (size - 1) // 2
            for far in range(1, ups + 1):
                on = [(1, after, True)] if far < ups else []
                self.arrivals.append((lax.rem(at + size - far, size), True, on))
                if far <= downs:
                    on = [(0, before, True)] if far < downs else []
                    self.arrivals.append((lax.rem(at + far, size), True, on))


def gather_kernel(
    sizes, panel_ref, coulomb_ref, orbitals_ref, decay_ref, polar_ref, block_ref,
    full, own, lhs, local_sem, ici_sem, par_sem, snd_sem,
):
    ny, nx, nz = sizes
    tm, pts = lax.axis_index("tm"), lax.axis_index("pts")
    core = lax.rem(pts, 2)
    here = {"y": lax.div(tm, nx), "x": lax.rem(tm, nx), "z": lax.div(pts, 2)}
    lines = {"y": Line(here["y"], ny), "x": Line(here["x"], nx), "z": Line(here["z"], nz)}
    base = {"y": 1, "x": 3, "z": 5}
    shard = panel_ref.shape[0]
    half = shard // 2
    bands = panel_ref.shape[1]
    times = decay_ref.shape[0]
    rows = own.shape[0]
    orders = (("z", "x", "y"), ("z", "y", "x"))

    def device(at, on):
        return {"tm": at["y"] * nx + at["x"], "pts": at["z"] * 2 + on}

    def chip(at):
        return (at["y"] * nx + at["x"]) * nz + at["z"]

    def piece(stream, at, on):
        start = (chip(at) * 2 + on) * shard + stream * half
        return full.at[pl.ds(pl.multiple_of(start, half), half), :]

    def ici_copy(stream, at, axis, slot, to):
        target = dict(here)
        target[axis] = to
        return pltpu.make_async_remote_copy(
            src_ref=piece(stream, at, core), dst_ref=piece(stream, at, core),
            send_sem=snd_sem.at[stream, chip(at), base[axis] + slot],
            recv_sem=ici_sem.at[stream, chip(at)],
            device_id=device(target, core), device_id_type=MESH,
        )

    def partner_copy(stream, at, on):
        return pltpu.make_async_remote_copy(
            src_ref=piece(stream, at, on), dst_ref=piece(stream, at, on),
            send_sem=snd_sem.at[stream, chip(at), 0],
            recv_sem=par_sem.at[stream, chip(at)],
            device_id=device(here, 1 - core), device_id_type=MESH,
        )

    own_orbitals = pltpu.make_async_copy(
        orbitals_ref.at[pl.ds(pl.multiple_of(tm * rows, rows), rows), :], own, local_sem.at[0])
    mine = (chip(here) * 2 + core) * shard
    mine_rows = pl.ds(pl.multiple_of(mine, shard), shard)
    own_panel = pltpu.make_async_copy(panel_ref, full.at[mine_rows, :bands], local_sem.at[1])
    own_coulomb = pltpu.make_async_copy(coulomb_ref, full.at[mine_rows, bands:], local_sem.at[2])
    own_panel.start()
    own_coulomb.start()
    own_orbitals.start()

    barrier = pltpu.get_barrier_semaphore()
    peers = [(device(here, 1 - core), True)]
    for axis in "yxz":
        for _, to, valid in lines[axis].sends:
            target = dict(here)
            target[axis] = to
            peers.append((device(target, core), valid))
    for to, valid in peers:
        when(valid, lambda to=to: pl.semaphore_signal(barrier, inc=1, device_id=to, device_id_type=MESH))
    greeted = 1
    for line in lines.values():
        greeted = greeted + line.peers
    pl.semaphore_wait(barrier, greeted)

    own_panel.wait()
    own_coulomb.wait()

    sent = []

    def forward(stream, at, valid, hops):
        for axis, slot, to, ok in hops:
            when(ok, lambda axis=axis, slot=slot, to=to: ici_copy(stream, at, axis, slot, to).start())
        partner_copy(stream, at, core).start()

    def note(stream, at, valid, hops):
        for axis, slot, to, ok in hops:
            sent.append((stream, at, axis, slot, to, both(valid, ok)))

    def later(order, place):
        return [(axis, slot, to, ok) for axis in order[place:] for slot, to, ok in lines[axis].sends]

    def take(stream, at, valid, order, place, on):
        hops = [(order[place], slot, to, ok) for slot, to, ok in on] + later(order, place + 1)

        def run():
            ici_copy(stream, at, order[place], 0, here[order[place]]).wait_recv()
            forward(stream, at, valid, hops)

        note(stream, at, valid, hops)
        when(valid, run)

    for stream, order in enumerate(orders):
        note(stream, dict(here), True, later(order, 0))
        forward(stream, dict(here), True, later(order, 0))

    own_orbitals.wait()
    lanes = 512

    def scale(t, carry):
        for start in range(0, bands, lanes):
            cut = slice(start, start + lanes)
            value = own[:, cut].astype(jnp.float32) * decay_ref[pl.ds(t, 1), cut]
            lhs[pl.ds(pl.multiple_of(t * rows, rows), rows), cut] = value.astype(jnp.bfloat16)
        return carry

    lax.fori_loop(0, times, scale, 0)

    def with_axis(at, axis, to):
        moved = dict(at)
        moved[axis] = to
        return moved

    first = [(dict(here), True)]
    for to, valid, on in lines["z"].arrivals:
        at = with_axis(here, "z", to)
        for stream, order in enumerate(orders):
            take(stream, at, valid, order, 0, on)
        first.append((at, valid))

    columns = 2 * nz * shard

    def column_ready(y, x):
        for z in range(nz):
            at = {"y": y, "x": x, "z": z}
            for stream in range(2):
                partner_copy(stream, at, 1 - core).wait_recv()

    def compute(y, x):
        column_ready(y, x)
        group = y * nx + x
        cut = pl.ds(pl.multiple_of(group * columns, columns), columns)
        pltpu.make_async_copy(full.at[cut, bands:], block_ref.at[cut, :], local_sem.at[3 + group]).start()
        contract = (((1,), (1,)), ((), ()))

        def one(t, carry):
            mine = pl.ds(pl.multiple_of(t * rows, rows), rows)
            occ = lax.dot_general(lhs[mine, :NOCC], full[cut, :NOCC], contract,
                                  preferred_element_type=jnp.float32)
            vir = lax.dot_general(lhs[mine, NOCC:], full[cut, NOCC:bands], contract,
                                  preferred_element_type=jnp.float32)
            polar_ref[mine, cut] = (-(occ * vir)).astype(jnp.bfloat16)
            return carry

        lax.fori_loop(0, times, one, 0)

    compute(here["y"], here["x"])

    arrivals = [(axis, *entry) for axis in ("x", "y") for entry in lines[axis].arrivals]
    for at0, valid0 in first:
        for axis, to, valid, on in arrivals:
            at = with_axis(at0, axis, to)
            for stream, order in enumerate(orders):
                take(stream, at, both(valid0, valid), order, order.index(axis), on)
    for axis, to, valid, on in arrivals:
        when(valid, lambda axis=axis, to=to: compute(
            to if axis == "y" else here["y"], to if axis == "x" else here["x"]))
    for at0, valid0 in first:
        for y, valid1, on_y in lines["y"].arrivals:
            for x, valid2, on_x in lines["x"].arrivals:
                at = with_axis(with_axis(at0, "y", y), "x", x)
                valid = both(valid0, both(valid1, valid2))
                take(0, at, valid, orders[0], 2, on_y)
                take(1, at, valid, orders[1], 2, on_x)
    for y, valid1, _ in lines["y"].arrivals:
        for x, valid2, _ in lines["x"].arrivals:
            when(both(valid1, valid2), lambda y=y, x=x: compute(y, x))

    for stream, at, axis, slot, to, valid in sent:
        when(valid, lambda stream=stream, at=at, axis=axis, slot=slot, to=to:
             ici_copy(stream, at, axis, slot, to).wait_send())
    for y in range(ny):
        for x in range(nx):
            for z in range(nz):
                for stream in range(2):
                    partner_copy(stream, {"y": y, "x": x, "z": z}, core).wait_send()
    group = pl.ds(0, columns)
    for slot in range(ny * nx):
        pltpu.make_async_copy(full.at[group, bands:], block_ref.at[group, :], local_sem.at[3 + slot]).wait()


def finish_kernel(times, freqs, cosines_ref, polar_ref, block_ref, out_ref):
    parts = [
        jnp.dot(polar_ref[t], block_ref[...], preferred_element_type=jnp.float32) for t in range(times)
    ]
    for k in range(freqs):
        total = cosines_ref[k, 0] * parts[0]
        for t in range(1, times):
            total = total + cosines_ref[k, t] * parts[t]
        out_ref[k] = total.astype(out_ref.dtype)


def shards(sizes, orbitals, panel_orbitals, band_gap, tau_points, quad_weight, frequencies, coulomb):
    times = tau_points.shape[0]
    freqs = frequencies.shape[0]
    groups = lax.axis_size("tm")
    devices = groups * lax.axis_size("pts")
    bands = orbitals.shape[1]
    rows = orbitals.shape[0] // groups
    shard = panel_orbitals.shape[0]
    panel = shard * devices
    width = coulomb.shape[1]
    chips = devices // 2
    decay = jnp.exp(-band_gap[None, :] * tau_points[:, None])
    cosines = quad_weight[None, :] * jnp.cos(frequencies[:, None] * tau_points[None, :])
    hbm = pl.BlockSpec(memory_space=pl.ANY)
    vmem = pl.BlockSpec(memory_space=pltpu.VMEM)
    polar, block = pl.pallas_call(
        functools.partial(gather_kernel, sizes),
        out_shape=(
            jax.ShapeDtypeStruct((times * rows, panel), jnp.bfloat16),
            jax.ShapeDtypeStruct((panel, width), jnp.bfloat16),
        ),
        in_specs=[hbm, hbm, hbm, vmem],
        out_specs=(vmem, hbm),
        scratch_shapes=[
            pltpu.VMEM((panel, bands + width), jnp.bfloat16),
            pltpu.VMEM((rows, bands), jnp.bfloat16),
            pltpu.VMEM((times * rows, bands), jnp.bfloat16),
            pltpu.SemaphoreType.DMA((3 + groups,)),
            pltpu.SemaphoreType.DMA((2, chips)),
            pltpu.SemaphoreType.DMA((2, chips)),
            pltpu.SemaphoreType.DMA((2, chips, DIRS)),
        ],
        compiler_params=pltpu.CompilerParams(
            collective_id=0, has_side_effects=True, vmem_limit_bytes=48 * 1024 * 1024
        ),
        name="gather_polar",
    )(panel_orbitals, coulomb, orbitals, decay)
    tile = min(rows, 128)
    wide = min(width, 256)
    return pl.pallas_call(
        functools.partial(finish_kernel, times, freqs),
        grid=(rows // tile, width // wide),
        out_shape=jax.ShapeDtypeStruct((freqs, rows, width), jnp.bfloat16),
        in_specs=[
            pl.BlockSpec(memory_space=pltpu.SMEM),
            pl.BlockSpec((times, tile, panel), lambda i, j: (0, i, 0)),
            pl.BlockSpec((panel, wide), lambda i, j: (0, j)),
        ],
        out_specs=pl.BlockSpec((freqs, tile, wide), lambda i, j: (0, i, j)),
        compiler_params=pltpu.CompilerParams(vmem_limit_bytes=48 * 1024 * 1024),
        name="screen",
    )(cosines, polar.reshape(times, rows, panel), block)


def solution(mesh):
    groups, points = mesh.shape["tm"], mesh.shape["pts"]
    sizes = (groups // 2, 2, points // 2)
    placed = (P("pts", None), P(("tm", "pts"), None), P(), P(), P(), P(), P(("tm", "pts"), None))
    return jax.shard_map(
        functools.partial(shards, sizes), mesh=mesh, in_specs=placed,
        out_specs=P(None, ("pts", "tm"), None), check_vma=False,
    )
```

time: 155 us -> 49.4 us (0.32)
  waiting for transfers between devices: 111 us -> 0 us
  Pallas kernels: 0 us -> 44.8 us
  matrix products: 17.1 us -> 0 us
  between operations: 13.4 us -> 0.02 us
  other arithmetic: 10.3 us -> 2.24 us
    all_gather x2 -> x0, waiting for transfers between devices: 110 us -> none  [the longest x1 59.7 us: shards(): panel = lax.all_gather(panel_orbitals, ('tm', 'pts'), axis=0, tiled=True)]
    pallas_call x0 -> x2, Pallas kernels: none -> 44.8 us  [the longest x1 37.2 us: shards(): pl.pallas_call(functools.partial(gather_kernel, sizes), out_shape=(jax.Sh...]
    dot_general x2 -> x0, matrix products: 17.1 us -> none  [the longest x1 8.88 us: shards(): product = jnp.dot(polar, block, preferred_element_type=jnp.float32)]
    convert_element_type x3 -> x0, other arithmetic: 8.09 us -> none  [the longest x1 3.58 us: shards(): return total.astype(jnp.bfloat16)]
    slice x1 -> x0, local copies, waits for them, and re-layouts: 2.48 us -> none  [shards(): total = cosines[:, 0, None, None] * product[None, 0]]
    unnamed x0 -> x4, local copies, waits for them, and re-layouts: none -> 1.74 us
  transfers between devices with their start and end apart: 2 -> 0, of which waited for: 2 -> 0; matrix products, arithmetic and copies ran while one was open for 10% -> 0% of each run, Pallas kernels for 0% -> 0%
where the time goes in v2:
time: 49.4 us; the launch traced here: 48.8 us
  Pallas kernels  44.8 us (91%)
  other arithmetic  2.24 us (5%)
  local copies, waits for them, and re-layouts  1.74 us (4%)
    pallas_call x1, Pallas kernels, shards(): pl.pallas_call(functools.partial(gather_kernel, sizes), out_shape=(jax.Sh...  37.2 us
    pallas_call x1, Pallas kernels, shards(): pl.pallas_call(functools.partial(finish_kernel, times, freqs), grid=(rows...  7.6 us
    unnamed x4, local copies, waits for them, and re-layouts  1.74 us

profile of v2, /device:TPU:1, one launch (start us, length us, event | category | flops | bytes accessed | tf_op | source)
XLA Modules:
  0.0 48.8 jit_solution(13472394881280872654)
XLA Ops:
  0.0 0.8 %cosine_multiply_fusion.cosines_ref = f32[8,4]{1,0:T(8,128)S(1)} fusion(f32[4]{0:T(128)} %param.10, f32[8]{0:T(128)} %param.12, f32[4]{0:T(128)} %param.11), kind=kLoop, calls=%fused_computation.1 | loop fusion | flops 64 | bytes 192 | tf_op jit(solution)/shard_map/mul | solution.py:271
  0.8 0.7 %neg.4 = f32[2048]{0:T(1024)S(1)} negate(f32[2048]{0:T(1024)} %param.9) | non-fusion elementwise | flops 2048 | bytes 16384 | tf_op jit(solution)/shard_map/neg | solution.py:270
  1.5 0.7 %multiply_exponential_fusion.decay_ref = f32[4,2048]{1,0:T(4,128)S(1)} fusion(f32[4]{0:T(128)} %param.10, f32[2048]{0:T(1024)S(1)} %neg.4), kind=kLoop, calls=%fused_computation | loop fusion | flops 8192 | bytes 40976 | tf_op jit(solution)/shard_map/exp | solution.py:270
  2.2 0.0 copy-start
  2.3 0.9 %copy-done = bf16[32,2048]{1,0:T(8,128)(2,1)S(1)} copy-done((bf16[32,2048]{1,0:T(8,128)(2,1)S(1)}, bf16[32,2048]{1,0:T(8,128)(2,1)}, u32[]{:S(2)}) %copy-start) | copy-done | bytes 131096
  3.1 0.0 copy-start.1
  3.2 0.8 %copy-done.1 = bf16[32,1024]{1,0:T(8,128)(2,1)S(1)} copy-done((bf16[32,1024]{1,0:T(8,128)(2,1)S(1)}, bf16[32,1024]{1,0:T(8,128)(2,1)}, u32[]{:S(2)}) %copy-start.1) | copy-done | bytes 65560
  4.0 37.2 %gather_polar.1 = (bf16[1024,1024]{1,0:T(8,128)(2,1)S(1)}, bf16[1024,1024]{1,0:T(8,128)(2,1)S(1)}) custom-call(bf16[32,2048]{1,0:T(8,128)(2,1)S(1)} %copy-done, bf16[32,1024]{1,0:T(8,128)(2,1)S(1)} %copy-done.1, bf16[1024,2048]{1,0:T(8,128)(2,1)} %orbitals_ref.1, f32[4,2048]{1,0:T(4,128)S(1)} %multiply_exponential_fusion.decay_ref), custom_call_target="tpu_custom_call" | custom-call | tf_op jit(solution)/shard_map/gather_polar/pallas_call | solution.py:274
  41.2 7.6 %screen.1 = bf16[8,256,1024]{2,1,0:T(8,128)(2,1)} custom-call(f32[8,4]{1,0:T(8,128)S(1)} %cosine_multiply_fusion.cosines_ref, bf16[4,256,1024]{2,1,0:T(8,128)(2,1)S(1)} %bitcast.1, bf16[1024,1024]{1,0:T(8,128)(2,1)S(1)} %get-tuple-element.8.block_ref), custom_call_target="tpu_custom_call" | custom-call | tf_op jit(solution)/shard_map/screen/pallas_call | solution.py:298
Async XLA Ops:
  2.2 0.9 %copy-start = (bf16[32,2048]{1,0:T(8,128)(2,1)S(1)}, bf16[32,2048]{1,0:T(8,128)(2,1)}, u32[]{:S(2)}) copy-start(bf16[32,2048]{1,0:T(8,128)(2,1)} %panel_ref.1) | copy-start | bytes 393220
  3.1 0.8 %copy-start.1 = (bf16[32,1024]{1,0:T(8,128)(2,1)S(1)}, bf16[32,1024]{1,0:T(8,128)(2,1)}, u32[]{:S(2)}) copy-start(bf16[32,1024]{1,0:T(8,128)(2,1)} %coulomb_ref.1) | copy-start | bytes 196612

commit v3 on v1

--- a/solution.py
+++ b/solution.py
@@ -1,9 +1,345 @@
+import functools
 import jax
 import jax.numpy as jnp
 from jax import lax
+from jax.experimental import pallas as pl
+from jax.experimental.pallas import tpu as pltpu
 from jax.sharding import PartitionSpec as P
 
 NOCC = 512
+MESH = pl.DeviceIdType.MESH
+LANES = 128
+
+
+def when(valid, run):
+    if valid is True:
+        run()
+    elif valid is not False:
+        pl.when(valid)(run)
+
+
+def both(a, b):
+    if a is True:
+        return b
+    if b is True:
+        return a
+    if a is False or b is False:
+        return False
+    return jnp.logical_and(a, b)
+
+
+class Line:
+    def __init__(self, at, size):
+        self.at, self.size = at, size
+        if size == 1:
+            self.sends, self.arrivals, self.peers = [], [], 0
+        elif size == 2:
+            other = 1 - at
+            self.peers = 1
+            self.sends = [(0, other, True)]
+            self.arrivals = [(other, True, [])]
+        elif size <= 4:
+            down, up = at > 0, at < size - 1
+            self.peers = lax.div(at + size - 1, size) + lax.div(2 * size - 2 - at, size)
+            self.sends = [(0, at - 1, down), (1, at + 1, up)]
+            self.arrivals = []
+            for far in range(1, size):
+                self.arrivals.append((at - far, at >= far, [(1, at + 1, up)]))
+                self.arrivals.append((at + far, at < size - far, [(0, at - 1, down)]))
+        else:
+            before, after = lax.rem(at + size - 1, size), lax.rem(at + 1, size)
+            self.sends = [(0, before, True), (1, after, True)]
+            self.peers = 2
+            self.arrivals = []
+            ups, downs = size // 2, (size - 1) // 2
+            for far in range(1, ups + 1):
+                on = [(1, after, True)] if far < ups else []
+                self.arrivals.append((lax.rem(at + size - far, size), True, on))
+                if far <= downs:
+                    on = [(0, before, True)] if far < downs else []
+                    self.arrivals.append((lax.rem(at + far, size), True, on))
+
+
+def gather_kernel(
+    sizes, panel_ref, coulomb_ref, orbitals_ref, band_ref, tau_ref, weight_ref, freq_ref, sum_ref, cos_ref,
+    panel, block, own, lhs, local_sem, ici_sem, par_sem, snd_sem,
+):
+    ny, nx, nz = sizes
+    tm, pts = lax.axis_index("tm"), lax.axis_index("pts")
+    core = lax.rem(pts, 2)
+    here = {"y": lax.div(tm, nx), "x": lax.rem(tm, nx), "z": lax.div(pts, 2)}
+    lines = {"y": Line(here["y"], ny), "x": Line(here["x"], nx), "z": Line(here["z"], nz)}
+    base = {"y": 1, "x": 1 + slots(ny), "z": 1 + slots(ny) + slots(nx)}
+    shard = panel_ref.shape[0]
+    half = shard // 2
+    bands = panel_ref.shape[1]
+    times = tau_ref.shape[0]
+    freqs = freq_ref.shape[0]
+    rows = own.shape[0]
+    streams = (
+        (panel, 0, ("x", "z", "y")), (panel, 1, ("y", "z", "x")),
+        (block, 0, ("z", "x", "y")), (block, 1, ("z", "y", "x")),
+    )
+    kinds = range(len(streams))
+
+    def device(at, on):
+        return {"tm": at["y"] * nx + at["x"], "pts": at["z"] * 2 + on}
+
+    def chip(at):
+        return (at["y"] * nx + at["x"]) * nz + at["z"]
+
+    def piece(kind, at, on):
+        array, part, _ = streams[kind]
+        start = (chip(at) * 2 + on) * shard + part * half
+        return array.at[pl.ds(pl.multiple_of(start, half), half), :]
+
+    def moved(at, axis, to):
+        other = dict(at)
+        other[axis] = to
+        return other
+
+    def ici_copy(kind, at, axis, slot, to):
+        return pltpu.make_async_remote_copy(
+            src_ref=piece(kind, at, core), dst_ref=piece(kind, at, core),
+            send_sem=snd_sem.at[kind, chip(at), base[axis] + slot],
+            recv_sem=ici_sem.at[kind, chip(at)],
+            device_id=device(moved(here, axis, to), core), device_id_type=MESH,
+        )
+
+    def partner_copy(kind, at, on):
+        return pltpu.make_async_remote_copy(
+            src_ref=piece(kind, at, on), dst_ref=piece(kind, at, on),
+            send_sem=snd_sem.at[kind, chip(at), 0],
+            recv_sem=par_sem.at[kind, chip(at)],
+            device_id=device(here, 1 - core), device_id_type=MESH,
+        )
+
+    own_orbitals = pltpu.make_async_copy(
+        orbitals_ref.at[pl.ds(pl.multiple_of(tm * rows, rows), rows), :], own, local_sem.at[0])
+    mine = (chip(here) * 2 + core) * shard
+    mine_rows = pl.ds(pl.multiple_of(mine, shard), shard)
+    own_panel = pltpu.make_async_copy(panel_ref, panel.at[mine_rows, :], local_sem.at[1])
+    own_coulomb = pltpu.make_async_copy(coulomb_ref, block.at[mine_rows, :], local_sem.at[2])
+    own_panel.start()
+    own_coulomb.start()
+    own_orbitals.start()
+
+    barrier = pltpu.get_barrier_semaphore()
+    peers = [(device(here, 1 - core), True)]
+    greeted = 1
+    for axis, line in lines.items():
+        greeted = greeted + line.peers
+        for _, to, valid in line.sends:
+            peers.append((device(moved(here, axis, to), core), valid))
+    for to, valid in peers:
+        when(valid, lambda to=to: pl.semaphore_signal(barrier, inc=1, device_id=to, device_id_type=MESH))
+    pl.semaphore_wait(barrier, greeted)
+
+    own_panel.wait()
+    own_coulomb.wait()
+
+    sent = []
+
+    def forward(kind, at, hops):
+        for axis, slot, to, ok in hops:
+            when(ok, lambda axis=axis, slot=slot, to=to: ici_copy(kind, at, axis, slot, to).start())
+        partner_copy(kind, at, core).start()
+
+    def note(kind, at, valid, hops):
+        for axis, slot, to, ok in hops:
+            sent.append((kind, at, axis, slot, to, both(valid, ok)))
+
+    def later(order, place):
+        return [(axis, slot, to, ok) for axis in order[place:] for slot, to, ok in lines[axis].sends]
+
+    def take(kind, entries):
+        order = streams[kind][2]
+        place = max(order.index(axis) for axis in entries)
+        at, valid = dict(here), True
+        for axis, (to, ok, _) in entries.items():
+            at[axis] = to
+            valid = both(valid, ok)
+        last = order[place]
+        hops = [(last, slot, to, ok) for slot, to, ok in entries[last][2]] + later(order, place + 1)
+
+        def run():
+            ici_copy(kind, at, last, 0, here[last]).wait_recv()
+            forward(kind, at, hops)
+
+        note(kind, at, valid, hops)
+        when(valid, run)
+
+    for kind in kinds:
+        hops = later(streams[kind][2], 0)
+        note(kind, dict(here), True, hops)
+        forward(kind, dict(here), hops)
+
+    own_orbitals.wait()
+    gap = band_ref[...]
+    for t in range(times):
+        decay = jnp.exp(-gap * tau_ref[t])
+        cut = slice(t * rows, (t + 1) * rows)
+        for start in range(0, bands, 512):
+            wide = slice(start, start + 512)
+            value = own[:, wide].astype(jnp.float32) * decay[:, wide]
+            lhs[cut, wide] = value.astype(jnp.bfloat16)
+    place = lax.broadcasted_iota(jnp.int32, (freqs, LANES), 0)
+    freq = jnp.zeros((freqs, LANES), jnp.float32)
+    for k in range(freqs):
+        freq = jnp.where(place == k, freq_ref[k], freq)
+    for t in range(times):
+        cos_ref[t] = weight_ref[t] * jnp.cos(freq * tau_ref[t])
+
+    columns = 2 * nz * shard
+    work = []
+
+    def compute(y, x, valid, fresh):
+        group = y * nx + x
+        cut = pl.ds(pl.multiple_of(group * columns, columns), columns)
+        contract = (((1,), (1,)), ((), ()))
+
+        def one(t):
+            if t == 0:
+                for z in range(nz):
+                    for kind in kinds:
+                        partner_copy(kind, {"y": y, "x": x, "z": z}, 1 - core).wait_recv()
+            mine = slice(t * rows, (t + 1) * rows)
+            occ = lax.dot_general(lhs[mine, :NOCC], panel[cut, :NOCC], contract,
+                                  preferred_element_type=jnp.float32)
+            vir = lax.dot_general(lhs[mine, NOCC:], panel[cut, NOCC:], contract,
+                                  preferred_element_type=jnp.float32)
+            polar = (-(occ * vir)).astype(jnp.bfloat16)
+            term = jnp.dot(polar, block[cut, :], preferred_element_type=jnp.float32)
+            if fresh:
+                sum_ref[mine, :] = term
+            else:
+                sum_ref[mine, :] += term
+
+        for t in range(times):
+            work.append((valid, functools.partial(one, t)))
+
+    def step():
+        if work:
+            valid, run = work.pop(0)
+            when(valid, run)
+
+    def take_sides(entries):
+        for kind in kinds:
+            for axis in ("x", "y"):
+                for entry in lines[axis].arrivals:
+                    take(kind, {**entries, axis: entry})
+
+    along = lines["z"].arrivals
+    batches = [along[i:i + 2] for i in range(0, len(along), 2)]
+    ahead = [{}]
+    for batch in batches:
+        for entry in batch:
+            for kind in kinds:
+                take(kind, {"z": entry})
+        for entries in ahead:
+            take_sides(entries)
+        ahead = [{"z": entry} for entry in batch]
+    compute(here["y"], here["x"], True, True)
+    for entries in ahead:
+        take_sides(entries)
+    step()
+    for axis in ("x", "y"):
+        for to, valid, _ in lines[axis].arrivals:
+            compute(to if axis == "y" else here["y"], to if axis == "x" else here["x"], valid, False)
+    steps = -(-len(work) // (1 + len(along)))
+    for entries in [{}] + [{"z": entry} for entry in along]:
+        for y in lines["y"].arrivals:
+            for x in lines["x"].arrivals:
+                for kind in kinds:
+                    take(kind, {**entries, "y": y, "x": x})
+        for _ in range(steps):
+            step()
+    for y, valid1, _ in lines["y"].arrivals:
+        for x, valid2, _ in lines["x"].arrivals:
+            compute(y, x, both(valid1, valid2), False)
+    while work:
+        step()
+
+    for kind, at, axis, slot, to, valid in sent:
+        when(valid, lambda kind=kind, at=at, axis=axis, slot=slot, to=to:
+             ici_copy(kind, at, axis, slot, to).wait_send())
+    for y in range(ny):
+        for x in range(nx):
+            for z in range(nz):
+                for kind in kinds:
+                    partner_copy(kind, {"y": y, "x": x, "z": z}, core).wait_send()
+
+
+def finish_kernel(times, freqs, cos_ref, sum_ref, out_ref):
+    tile = 16
+    weights = [[cos_ref[t, k:k + 1, 0:1] for t in range(times)] for k in range(freqs)]
+
+    def some(i, carry):
+        cut = pl.ds(pl.multiple_of(i * tile, tile), tile)
+        parts = [sum_ref[t, cut, :] for t in range(times)]
+        for k in range(freqs):
+            total = weights[k][0] * parts[0]
+            for t in range(1, times):
+                total = total + weights[k][t] * parts[t]
+            out_ref[k, cut, :] = total.astype(out_ref.dtype)
+        return carry
+
+    lax.fori_loop(0, sum_ref.shape[1] // tile, some, 0)
+
+
+def slots(size):
+    return min(size - 1, 2)
+
+
+def shards(sizes, orbitals, panel_orbitals, band_gap, tau_points, quad_weight, frequencies, coulomb):
+    times = tau_points.shape[0]
+    freqs = frequencies.shape[0]
+    groups = lax.axis_size("tm")
+    devices = groups * lax.axis_size("pts")
+    bands = orbitals.shape[1]
+    rows = orbitals.shape[0] // groups
+    panel = panel_orbitals.shape[0] * devices
+    width = coulomb.shape[1]
+    chips = devices // 2
+    hbm = pl.BlockSpec(memory_space=pltpu.HBM)
+    vmem = pl.BlockSpec(memory_space=pltpu.VMEM)
+    smem = pl.BlockSpec(memory_space=pltpu.SMEM)
+    sums, cosines = pl.pallas_call(
+        functools.partial(gather_kernel, sizes),
+        out_shape=(
+            jax.ShapeDtypeStruct((times * rows, width), jnp.float32),
+            jax.ShapeDtypeStruct((times, freqs, LANES), jnp.float32),
+        ),
+        in_specs=[hbm, hbm, hbm, vmem, smem, smem, smem],
+        out_specs=(vmem, vmem),
+        scratch_shapes=[
+            pltpu.VMEM((panel, bands), jnp.bfloat16),
+            pltpu.VMEM((panel, width), jnp.bfloat16),
+            pltpu.VMEM((rows, bands), jnp.bfloat16),
+            pltpu.VMEM((times * rows, bands), jnp.bfloat16),
+            pltpu.SemaphoreType.DMA((3,)),
+            pltpu.SemaphoreType.DMA((4, chips)),
+            pltpu.SemaphoreType.DMA((4, chips)),
+            pltpu.SemaphoreType.DMA((4, chips, 1 + sum(slots(size) for size in sizes))),
+        ],
+        compiler_params=pltpu.CompilerParams(
+            collective_id=0, has_side_effects=True, vmem_limit_bytes=62824448
+        ),
+        name="gather_sum",
+    )(panel_orbitals, coulomb, orbitals, band_gap.reshape(1, bands), tau_points, quad_weight, frequencies)
+    tile = min(rows, 64)
+    return pl.pallas_call(
+        functools.partial(finish_kernel, times, freqs),
+        grid=(rows // tile,),
+        out_shape=jax.ShapeDtypeStruct((freqs, rows, width), jnp.bfloat16),
+        in_specs=[
+            pl.BlockSpec((times, freqs, LANES), lambda i: (0, 0, 0)),
+            pl.BlockSpec((times, tile, width), lambda i: (0, i, 0)),
+        ],
+        out_specs=pl.BlockSpec((freqs, tile, width), lambda i: (0, i, 0)),
+        compiler_params=pltpu.CompilerParams(vmem_limit_bytes=62824448),
+        name="finish",
+    )(cosines, sums.reshape(times, rows, width))
 
 
 def contract(left, right):
@@ -12,7 +348,7 @@
     )
 
 
-def shards(orbitals, panel_orbitals, band_gap, tau_points, quad_weight, frequencies, coulomb):
+def many_shards(orbitals, panel_orbitals, band_gap, tau_points, quad_weight, frequencies, coulomb):
     times = tau_points.shape[0]
     rows = orbitals.shape[0] // lax.axis_size("tm")
     own = lax.dynamic_slice_in_dim(orbitals, lax.axis_index("tm") * rows, rows)
@@ -34,7 +370,11 @@
 
 
 def solution(mesh):
+    groups, points = mesh.shape["tm"], mesh.shape["pts"]
+    sizes = (groups // 2, 2, points // 2)
     placed = (P("pts", None), P(("tm", "pts"), None), P(), P(), P(), P(), P(("tm", "pts"), None))
+    local = functools.partial(shards, sizes) if groups * points <= 32 else many_shards
     return jax.shard_map(
-        shards, mesh=mesh, in_specs=placed, out_specs=P(None, ("pts", "tm"), None), check_vma=False
+        local, mesh=mesh, in_specs=placed,
+        out_specs=P(None, ("pts", "tm"), None), check_vma=False,
     )

time: 155 us -> 52.9 us (0.34)
  waiting for transfers between devices: 111 us -> 0 us
  Pallas kernels: 0 us -> 52.7 us
  matrix products: 17.1 us -> 0 us
  between operations: 13.4 us -> 0.01 us
  other arithmetic: 10.3 us -> 0 us
  local copies, waits for them, and re-layouts: 2.49 us -> 0 us
    all_gather x2 -> x0, waiting for transfers between devices: 110 us -> none  [the longest x1 59.7 us: shards(): panel = lax.all_gather(panel_orbitals, ('tm', 'pts'), axis=0, tiled=True)]
    pallas_call x0 -> x2, Pallas kernels: none -> 52.7 us  [the longest x1 46.7 us: shards(): pl.pallas_call(functools.partial(gather_kernel, sizes), out_shape=(jax.Sh...]
    dot_general x2 -> x0, matrix products: 17.1 us -> none  [the longest x1 8.88 us: shards(): product = jnp.dot(polar, block, preferred_element_type=jnp.float32)]
    convert_element_type x3 -> x0, other arithmetic: 8.09 us -> none  [the longest x1 3.58 us: shards(): return total.astype(jnp.bfloat16)]
    slice x1 -> x0, local copies, waits for them, and re-layouts: 2.48 us -> none  [shards(): total = cosines[:, 0, None, None] * product[None, 0]]
  transfers between devices with their start and end apart: 2 -> 0, of which waited for: 2 -> 0; matrix products, arithmetic and copies ran while one was open for 10% -> 0% of each run, Pallas kernels for 0% -> 0%
where the time goes in v3:
time: 52.9 us; the launch traced here: 52.7 us
  Pallas kernels  52.7 us (100%)
    pallas_call x1, Pallas kernels, shards(): pl.pallas_call(functools.partial(gather_kernel, sizes), out_shape=(jax.Sh...  46.7 us
    pallas_call x1, Pallas kernels, shards(): pl.pallas_call(functools.partial(finish_kernel, times, freqs), grid=(rows...  6.03 us

profile of v3, /device:TPU:1, one launch (start us, length us, event | category | flops | bytes accessed | tf_op | source)
XLA Modules:
  0.0 52.7 jit_solution(14440284787829563168)
XLA Ops:
  0.0 46.7 %gather_sum.1 = (f32[1024,1024]{1,0:T(8,128)}, f32[4,8,128]{2,1,0:T(8,128)}) custom-call(bf16[32,2048]{1,0:T(8,128)(2,1)} %panel_ref.1, bf16[32,1024]{1,0:T(8,128)(2,1)} %coulomb_ref.1, bf16[1024,2048]{1,0:T(8,128)(2,1)} %orbitals_ref.1, f32[1,2048]{1,0:T(1,128)} %bitcast.3, f32[4]{0:T(128)} %tau_ref.1, f32[4]{0:T(128)} %weight_ref.1, f32[8]{0:T(128)} %freq_ref.1), custom_call_target="tpu_custom_call" | custom-call | tf_op jit(solution)/shard_map/gather_sum/pallas_call | solution.py:307
  46.7 6.0 %finish.1 = bf16[8,256,1024]{2,1,0:T(8,128)(2,1)} custom-call(f32[4,8,128]{2,1,0:T(8,128)} %get-tuple-element.7.cos_ref, f32[4,256,1024]{2,1,0:T(8,128)} %bitcast.2), custom_call_target="tpu_custom_call" | custom-call | tf_op jit(solution)/shard_map/finish/pallas_call | solution.py:331
